TPU v7x, 256 devices: a whole 4x4x8 slice. The times are simulated.
256 devices in a mesh: ctx: 32 (over x, z), tp: 8 (over y, core).
Axes of the slice: x: 4, y: 4, z: 8, core: 2. Of those that a mesh axis runs over, the one named last changes fastest.
Arguments:
- projected: bfloat16 [4096, 3, 4096], P('ctx', None, 'tp'), may hold values from -6 to 6
- short_filter: float32 [7, 3, 4096], P(None, None, 'tp'), may hold values from -2.4 to 2.4
- long_filter: bfloat16 [256, 2048], P('tp'), may hold values from -0.26516504 to 0.26516504
- out_weight: bfloat16 [4096, 8192], P('tp'), may hold values from -0.09375 to 0.09375
Outputs:
- layer_out: bfloat16 [4096, 8192], P('ctx', 'tp')
All inputs are finite; a program needn't handle non-finite values.
Results may differ from a plain program's by a relative error of at most 0.015.
Values may be sent and summed in bfloat16 or wider, within the bound.
No kernel may reach another device: no remote copies, remote signals or barrier semaphores. Data moves between devices by JAX's collectives and lax.ppermute only.
A program may use at most 64 MiB of HBM per device.

v0:
```python
import math
import jax
import jax.numpy as jnp
from jax import lax
from jax.sharding import PartitionSpec as P


def shifted(array, axis, by):
    size = lax.axis_size(axis)
    pairs = [(i, i + by) for i in range(size) if 0 <= i + by < size]
    return lax.ppermute(array, axis, pairs)


def toeplitz_block(padded_taps, lag_base, count, tok_rows):
    width = tok_rows + count - 1
    groups = padded_taps.shape[0]
    window = lax.dynamic_slice_in_dim(padded_taps, lag_base - (count - 1) + 2 * tok_rows, width, 1)
    flipped = jnp.concatenate([window[:, ::-1], jnp.zeros((groups, 1), window.dtype)], axis=1)
    tiled = jnp.tile(flipped, (1, tok_rows))
    skewed = tiled[:, : tok_rows * width].reshape(groups, tok_rows, width)
    return skewed[:, :, tok_rows - 1 : tok_rows - 1 + count]


def block_term(padded_taps, source, lag_base, tok_rows):
    count, channels = source.shape
    groups = padded_taps.shape[0]
    matrix = toeplitz_block(padded_taps, lag_base, count, tok_rows)
    grouped = source.reshape(count, groups, channels // groups)
    term = jnp.einsum("gts,sgi->tgi", matrix, grouped, preferred_element_type=jnp.float32)
    return term.reshape(tok_rows, channels)


def add_blocks(total, piece, padded_taps, my_start, reach):
    tok_rows = total.shape[0]
    count = piece.shape[0]
    block = math.gcd(count, tok_rows)

    def one_block(index, carry):
        first = index * block
        source = lax.dynamic_slice_in_dim(piece, index * block, block, 0)
        lag_base = my_start - first
        useful = jnp.logical_and(lag_base + tok_rows - 1 >= 0, lag_base - block + 1 <= reach - 1)
        return lax.cond(
            useful,
            lambda running: running + block_term(padded_taps, source, lag_base, tok_rows),
            lambda running: running,
            carry,
        )

    return lax.fori_loop(0, count // block, one_block, total)


def body(projected, short_filter, long_filter, out_weight):
    tok_rows = projected.shape[0]
    taps = short_filter.shape[0]
    groups = long_filter.shape[0]
    reach = long_filter.shape[1]
    my_start = lax.axis_index("ctx") * tok_rows
    border = shifted(projected[tok_rows - (taps - 1) :], "ctx", 1)
    extended = jnp.concatenate([border, projected], axis=0).astype(jnp.float32)
    conved = short_filter[0] * extended[taps - 1 : taps - 1 + tok_rows]
    for offset in range(1, taps):
        conved = (
            conved
            + short_filter[offset] * extended[taps - 1 - offset : taps - 1 - offset + tok_rows]
        )
    values = (conved[:, 1, :] * conved[:, 2, :]).astype(jnp.bfloat16)
    padding = jnp.zeros((groups, 2 * tok_rows), long_filter.dtype)
    padded_taps = jnp.concatenate([padding, long_filter, padding], axis=1)
    empty = jnp.zeros(values.shape, jnp.float32)
    mixed = add_blocks(
        empty, lax.all_gather(values, "ctx", axis=0, tiled=True), padded_taps, my_start, reach
    )
    hidden = (conved[:, 0, :] * mixed).astype(jnp.bfloat16)
    partial_sum = jnp.dot(hidden, out_weight, preferred_element_type=jnp.float32)
    return lax.psum_scatter(partial_sum.astype(jnp.bfloat16), "tp", scatter_dimension=1, tiled=True)


def solution(mesh):
    return jax.shard_map(
        body,
        mesh=mesh,
        in_specs=(P("ctx", None, "tp"), P(None, None, "tp"), P("tp", None), P("tp", None)),
        out_specs=P("ctx", "tp"),
        check_vma=False,
    )
```

profile of v0, /device:TPU:2, one launch (start us, length us, event | category | flops | bytes accessed | tf_op | source)
XLA Modules:
  0.0 382.6 jit_solution(14550529410399828677)
XLA Ops:
  7.5 3.8 collective-permute-start
  13.9 10.5 %collective-permute-done = bf16[6,3,512]{0,2,1:T(8,128)(2,1)S(1)} collective-permute-done((bf16[6,3,512]{0,2,1:T(8,128)(2,1)S(1)}, bf16[6,3,512]{0,2,1:T(8,128)(2,1)S(1)}, u32[]{:S(2)}, u32[]{:S(2)}) %collective-permute-start) | collective-permute-done | bytes 18464 | tf_op jit(solution)/shard_map/ppermute | solution.py:11
  24.7 3.0 fusion.2
  28.5 83.2 %all-gather.3.cloned.1.call-done = bf16[4096,1,512]{0,2,1:T(8,128)(2,1)} async-done(((bf16[128,1,512]{0,2,1:T(8,128)(2,1)}), bf16[4096,1,512]{0,2,1:T(8,128)(2,1)}) %all-gather.3.cloned.1.call-update) | async-done | bytes 4194320 | tf_op jit(solution)/shard_map/all_gather | solution.py:72
  111.7 117.8 %while.20 = (s32[]{:T(128)}, f32[128,512]{0,1:T(8,128)S(1)}, s32[]{:T(128)}, bf16[32,2560]{1,0:T(8,128)(2,1)S(1)}, bf16[4096,512]{0,1:T(8,128)(2,1)}, /*index=5*...) while((s32[]{:T(128)}, f32[128,512]{0,1:T(8,128)S(1)}, s32[]{:T(128)}, ...), condition=%wide.region_3.0_spmd, body=%wide.region_0.0_spmd.sunk | while | flops 16842768 | bytes 17285120 | solution.py:50
  111.8 12.9 %conditional.2 = (f32[128,512]{0,1:T(8,128)S(1)}) conditional(s32[]{:T(128)} %convert_element_type.39, f32[128,512]{0,1:T(8,128)S(1)} %get-tuple-element.299, (s32[]{:T(128)}, bf16[32,2560]{1,0:T(8,128)(2,1)S(1)}, s32[]{:T(128)}, bf16[4096,512]{0,1:T(8,128)(2,1)}, f32[128,512]{0,1:T(8,128)S(1)}) %tuple.78), branch_computations={%region_1.0_spmd, %region_2.0_spmd} | conditional | flops 16842760 | bytes 17284898 | solution.py:43
  114.6 7.8 %reshape.15 = bf16[32,128,255]{2,1,0:T(8,128)(2,1)} reshape(bf16[32,32640]{1,0:T(8,128)(2,1)S(1)} %slice.80) | data formatting | bytes 4177920 | tf_op jit(solution)/shard_map/while/body/eval_jaxpr/cond/branch_1_fun/reshape | solution.py:20
  122.3 2.3 fusion
  124.7 12.9 %conditional.2 = (f32[128,512]{0,1:T(8,128)S(1)}) conditional(s32[]{:T(128)} %convert_element_type.39, f32[128,512]{0,1:T(8,128)S(1)} %get-tuple-element.299, (s32[]{:T(128)}, bf16[32,2560]{1,0:T(8,128)(2,1)S(1)}, s32[]{:T(128)}, bf16[4096,512]{0,1:T(8,128)(2,1)}, f32[128,512]{0,1:T(8,128)S(1)}) %tuple.78), branch_computations={%region_1.0_spmd, %region_2.0_spmd} | conditional | flops 16842760 | bytes 17284898 | solution.py:43
  127.5 7.8 %reshape.15 = bf16[32,128,255]{2,1,0:T(8,128)(2,1)} reshape(bf16[32,32640]{1,0:T(8,128)(2,1)S(1)} %slice.80) | data formatting | bytes 4177920 | tf_op jit(solution)/shard_map/while/body/eval_jaxpr/cond/branch_1_fun/reshape | solution.py:20
  135.3 2.3 fusion
  137.7 12.9 %conditional.2 = (f32[128,512]{0,1:T(8,128)S(1)}) conditional(s32[]{:T(128)} %convert_element_type.39, f32[128,512]{0,1:T(8,128)S(1)} %get-tuple-element.299, (s32[]{:T(128)}, bf16[32,2560]{1,0:T(8,128)(2,1)S(1)}, s32[]{:T(128)}, bf16[4096,512]{0,1:T(8,128)(2,1)}, f32[128,512]{0,1:T(8,128)S(1)}) %tuple.78), branch_computations={%region_1.0_spmd, %region_2.0_spmd} | conditional | flops 16842760 | bytes 17284898 | solution.py:43
  140.5 7.8 %reshape.15 = bf16[32,128,255]{2,1,0:T(8,128)(2,1)} reshape(bf16[32,32640]{1,0:T(8,128)(2,1)S(1)} %slice.80) | data formatting | bytes 4177920 | tf_op jit(solution)/shard_map/while/body/eval_jaxpr/cond/branch_1_fun/reshape | solution.py:20
  148.3 2.3 fusion
  150.7 12.9 %conditional.2 = (f32[128,512]{0,1:T(8,128)S(1)}) conditional(s32[]{:T(128)} %convert_element_type.39, f32[128,512]{0,1:T(8,128)S(1)} %get-tuple-element.299, (s32[]{:T(128)}, bf16[32,2560]{1,0:T(8,128)(2,1)S(1)}, s32[]{:T(128)}, bf16[4096,512]{0,1:T(8,128)(2,1)}, f32[128,512]{0,1:T(8,128)S(1)}) %tuple.78), branch_computations={%region_1.0_spmd, %region_2.0_spmd} | conditional | flops 16842760 | bytes 17284898 | solution.py:43
  153.5 7.8 %reshape.15 = bf16[32,128,255]{2,1,0:T(8,128)(2,1)} reshape(bf16[32,32640]{1,0:T(8,128)(2,1)S(1)} %slice.80) | data formatting | bytes 4177920 | tf_op jit(solution)/shard_map/while/body/eval_jaxpr/cond/branch_1_fun/reshape | solution.py:20
  161.3 2.3 fusion
  163.7 12.9 %conditional.2 = (f32[128,512]{0,1:T(8,128)S(1)}) conditional(s32[]{:T(128)} %convert_element_type.39, f32[128,512]{0,1:T(8,128)S(1)} %get-tuple-element.299, (s32[]{:T(128)}, bf16[32,2560]{1,0:T(8,128)(2,1)S(1)}, s32[]{:T(128)}, bf16[4096,512]{0,1:T(8,128)(2,1)}, f32[128,512]{0,1:T(8,128)S(1)}) %tuple.78), branch_computations={%region_1.0_spmd, %region_2.0_spmd} | conditional | flops 16842760 | bytes 17284898 | solution.py:43
  166.5 7.8 %reshape.15 = bf16[32,128,255]{2,1,0:T(8,128)(2,1)} reshape(bf16[32,32640]{1,0:T(8,128)(2,1)S(1)} %slice.80) | data formatting | bytes 4177920 | tf_op jit(solution)/shard_map/while/body/eval_jaxpr/cond/branch_1_fun/reshape | solution.py:20
  174.2 2.3 fusion
  176.6 12.9 %conditional.2 = (f32[128,512]{0,1:T(8,128)S(1)}) conditional(s32[]{:T(128)} %convert_element_type.39, f32[128,512]{0,1:T(8,128)S(1)} %get-tuple-element.299, (s32[]{:T(128)}, bf16[32,2560]{1,0:T(8,128)(2,1)S(1)}, s32[]{:T(128)}, bf16[4096,512]{0,1:T(8,128)(2,1)}, f32[128,512]{0,1:T(8,128)S(1)}) %tuple.78), branch_computations={%region_1.0_spmd, %region_2.0_spmd} | conditional | flops 16842760 | bytes 17284898 | solution.py:43
  179.4 7.8 %reshape.15 = bf16[32,128,255]{2,1,0:T(8,128)(2,1)} reshape(bf16[32,32640]{1,0:T(8,128)(2,1)S(1)} %slice.80) | data formatting | bytes 4177920 | tf_op jit(solution)/shard_map/while/body/eval_jaxpr/cond/branch_1_fun/reshape | solution.py:20
  187.2 2.3 fusion
  189.6 12.9 %conditional.2 = (f32[128,512]{0,1:T(8,128)S(1)}) conditional(s32[]{:T(128)} %convert_element_type.39, f32[128,512]{0,1:T(8,128)S(1)} %get-tuple-element.299, (s32[]{:T(128)}, bf16[32,2560]{1,0:T(8,128)(2,1)S(1)}, s32[]{:T(128)}, bf16[4096,512]{0,1:T(8,128)(2,1)}, f32[128,512]{0,1:T(8,128)S(1)}) %tuple.78), branch_computations={%region_1.0_spmd, %region_2.0_spmd} | conditional | flops 16842760 | bytes 17284898 | solution.py:43
  192.4 7.8 %reshape.15 = bf16[32,128,255]{2,1,0:T(8,128)(2,1)} reshape(bf16[32,32640]{1,0:T(8,128)(2,1)S(1)} %slice.80) | data formatting | bytes 4177920 | tf_op jit(solution)/shard_map/while/body/eval_jaxpr/cond/branch_1_fun/reshape | solution.py:20
  202.6 12.9 %conditional.2 = (f32[128,512]{0,1:T(8,128)S(1)}) conditional(s32[]{:T(128)} %convert_element_type.39, f32[128,512]{0,1:T(8,128)S(1)} %get-tuple-element.299, (s32[]{:T(128)}, bf16[32,2560]{1,0:T(8,128)(2,1)S(1)}, s32[]{:T(128)}, bf16[4096,512]{0,1:T(8,128)(2,1)}, f32[128,512]{0,1:T(8,128)S(1)}) %tuple.78), branch_computations={%region_1.0_spmd, %region_2.0_spmd} | conditional | flops 16842760 | bytes 17284898 | solution.py:43
  205.4 7.8 %reshape.15 = bf16[32,128,255]{2,1,0:T(8,128)(2,1)} reshape(bf16[32,32640]{1,0:T(8,128)(2,1)S(1)} %slice.80) | data formatting | bytes 4177920 | tf_op jit(solution)/shard_map/while/body/eval_jaxpr/cond/branch_1_fun/reshape | solution.py:20
  215.6 12.9 %conditional.2 = (f32[128,512]{0,1:T(8,128)S(1)}) conditional(s32[]{:T(128)} %convert_element_type.39, f32[128,512]{0,1:T(8,128)S(1)} %get-tuple-element.299, (s32[]{:T(128)}, bf16[32,2560]{1,0:T(8,128)(2,1)S(1)}, s32[]{:T(128)}, bf16[4096,512]{0,1:T(8,128)(2,1)}, f32[128,512]{0,1:T(8,128)S(1)}) %tuple.78), branch_computations={%region_1.0_spmd, %region_2.0_spmd} | conditional | flops 16842760 | bytes 17284898 | solution.py:43
  218.4 7.8 %reshape.15 = bf16[32,128,255]{2,1,0:T(8,128)(2,1)} reshape(bf16[32,32640]{1,0:T(8,128)(2,1)S(1)} %slice.80) | data formatting | bytes 4177920 | tf_op jit(solution)/shard_map/while/body/eval_jaxpr/cond/branch_1_fun/reshape | solution.py:20
  226.1 2.3 fusion
  229.5 6.0 %convolution_convert_fusion = bf16[128,8192]{1,0:T(8,128)(2,1)} fusion(bf16[512,8192]{1,0:T(8,128)(2,1)} %param.11, f32[128,512]{0,1:T(8,128)S(1)} %get-tuple-element.232, f32[128,3,512]{0,2,1:T(8,128)S(1)} %fusion.2), kind=kOutput, calls=%fused_computation.5 | convolution fusion | flops 1074921472 | bytes 11010048 | tf_op jit(solution)/shard_map/dot_general | solution.py:75
  235.6 140.2 %reduce-scatter.2.cloned.1.call-done = bf16[128,1024]{1,0:T(8,128)(2,1)} async-done(((bf16[128,8192]{1,0:T(8,128)(2,1)}), bf16[128,1024]{1,0:T(8,128)(2,1)}) %reduce-scatter.2.cloned.1.call-update) | async-done | bytes 262160 | tf_op jit(solution)/shard_map/reduce_scatter | solution.py:76
  (125 shorter events, 34.7 us)
Async XLA Ops:
  6.5 105.2 %all-gather.3.cloned.1.call-start = ((), (), s32[]{:S(2)}) async-start(), calls=%async_computation.2 | async-start | bytes 4325376 | tf_op jit(solution)/shard_map/all_gather | solution.py:72
  7.5 16.8 %collective-permute-start = (bf16[6,3,512]{0,2,1:T(8,128)(2,1)S(1)}, bf16[6,3,512]{0,2,1:T(8,128)(2,1)S(1)}, u32[]{:S(2)}, u32[]{:S(2)}) collective-permute-start(bf16[6,3,512]{0,2,1:T(8,128)(2,1)S(1)} %copy.7), channel_id=1, source_target_pairs={{0,8},{8,16},{16,24},{24,32},{32,40},{40,48},{48,56},{56,64},{64,7... | collective-permute-start | bytes 55304 | tf_op jit(solution)/shard_map/ppermute | solution.py:11
  24.7 3.8 copy-start
  28.4 347.4 %reduce-scatter.2.cloned.1.call-start = ((), (), s32[]{:S(2)}) async-start(), calls=%async_computation.1 | async-start | bytes 2359296 | tf_op jit(solution)/shard_map/reduce_scatter | solution.py:76
Sparse Core Ops, SparseCore 0:
  28.5 83.1 all-gather.2
  235.7 140.0 reduce-scatter.1
where the time goes:
time: 384 us; the launch traced here: 383 us
  waiting for transfers between devices  234 us (61%)
  local copies, waits for them, and re-layouts  98.2 us (26%)
  matrix products  26.7 us (7%)
  between operations  13.5 us (4%)
  other arithmetic  4.52 us (1%)
  starting transfers between devices  3.87 us (1%)
    reduce_scatter x1, waiting for transfers between devices, body(): lax.psum_scatter(partial_sum.astype(jnp.bfloat16), 'tp', scatter_dimensio...  140 us
    all_gather x1, waiting for transfers between devices, body(): lax.all_gather(values, 'ctx', axis=0, tiled=True)  83.2 us
    reshape x9, local copies, waits for them, and re-layouts, toeplitz_block(): skewed = tiled[:, :tok_rows * width].reshape(groups, tok_rows, width)  70 us
    dot_general x9, matrix products, block_term(): jnp.einsum('gts,sgi->tgi', matrix, grouped, preferred_element_type=jnp.fl...  20.7 us
    cond x27, local copies, waits for them, and re-layouts  13.1 us
    ppermute x1, waiting for transfers between devices, shifted(): return lax.ppermute(array, axis, pairs)  10.5 us
    dynamic_slice x9, local copies, waits for them, and re-layouts, one_block(): source = lax.dynamic_slice_in_dim(piece, index * block, block, 0)  8.29 us
  transfers between devices with their start and end apart: 3, of which 3 were waited for; matrix products, arithmetic and copies ran while one was open for 1% of the time, Pallas kernels for 0%

commit v1 on v0

--- a/solution.py
+++ b/solution.py
@@ -3,6 +3,14 @@
 import jax.numpy as jnp
 from jax import lax
 from jax.sharding import PartitionSpec as P
+
+
+def guide_axis_part(field_in):
+    reply = tuple((field_in for _ in range(lax.axis_size("ctx"))))
+    value_now = jnp.stack(reply)
+    built = lax.all_to_all(value_now, "ctx", concat_axis=0, split_axis=0)
+    tall = jnp.concatenate(built, axis=0)
+    return tall
 
 
 def shifted(array, axis, by):
@@ -68,9 +76,7 @@
     padding = jnp.zeros((groups, 2 * tok_rows), long_filter.dtype)
     padded_taps = jnp.concatenate([padding, long_filter, padding], axis=1)
     empty = jnp.zeros(values.shape, jnp.float32)
-    mixed = add_blocks(
-        empty, lax.all_gather(values, "ctx", axis=0, tiled=True), padded_taps, my_start, reach
-    )
+    mixed = add_blocks(empty, guide_axis_part(values), padded_taps, my_start, reach)
     hidden = (conved[:, 0, :] * mixed).astype(jnp.bfloat16)
     partial_sum = jnp.dot(hidden, out_weight, preferred_element_type=jnp.float32)
     return lax.psum_scatter(partial_sum.astype(jnp.bfloat16), "tp", scatter_dimension=1, tiled=True)

time: 384 us -> 419 us (1.091)
  local copies, waits for them, and re-layouts: 98.2 us -> 114 us
  waiting for transfers between devices: 234 us -> 245 us
  starting transfers between devices: 3.87 us -> 12.8 us
    all_to_all x0 -> x1, waiting for transfers between devices: none -> 92.8 us  [guide_axis_part(): built = lax.all_to_all(value_now, 'ctx', concat_axis=0, split_axis=0)]
    all_gather x1 -> x0, waiting for transfers between devices: 83.2 us -> none  [body(): lax.all_gather(values, 'ctx', axis=0, tiled=True)]
    all_to_all x0 -> x1, starting transfers between devices: none -> 8.92 us  [guide_axis_part(): built = lax.all_to_all(value_now, 'ctx', concat_axis=0, split_axis=0)]
    all_to_all x0 -> x1, local copies, waits for them, and re-layouts: none -> 6.5 us  [guide_axis_part(): built = lax.all_to_all(value_now, 'ctx', concat_axis=0, split_axis=0)]
    while x0 -> x1, local copies, waits for them, and re-layouts: none -> 6.41 us  [add_blocks(): return lax.fori_loop(0, count // block, one_block, total)]
where the time goes in v1:
time: 419 us; the launch traced here: 418 us
  waiting for transfers between devices  245 us (58%)
  local copies, waits for them, and re-layouts  114 us (27%)
  matrix products  26.8 us (6%)
  between operations  13.5 us (3%)
  starting transfers between devices  12.8 us (3%)
    reduce_scatter x1, waiting for transfers between devices, body(): lax.psum_scatter(partial_sum.astype(jnp.bfloat16), 'tp', scatter_dimensio...  141 us
    all_to_all x1, waiting for transfers between devices, guide_axis_part(): built = lax.all_to_all(value_now, 'ctx', concat_axis=0, split_axis=0)  92.8 us
    reshape x9, local copies, waits for them, and re-layouts, toeplitz_block(): skewed = tiled[:, :tok_rows * width].reshape(groups, tok_rows, width)  70 us
    dot_general x9, matrix products, block_term(): jnp.einsum('gts,sgi->tgi', matrix, grouped, preferred_element_type=jnp.fl...  20.7 us
    cond x27, local copies, waits for them, and re-layouts  13.1 us
    ppermute x1, waiting for transfers between devices, shifted(): return lax.ppermute(array, axis, pairs)  10.5 us
    all_to_all x1, starting transfers between devices, guide_axis_part(): built = lax.all_to_all(value_now, 'ctx', concat_axis=0, split_axis=0)  8.92 us
  transfers between devices with their start and end apart: 3, of which 3 were waited for; matrix products, arithmetic and copies ran while one was open for 1% of the time, Pallas kernels for 0%

profile of v1, /device:TPU:2, one launch (start us, length us, event | category | flops | bytes accessed | tf_op | source)
XLA Modules:
  0.0 417.6 jit_solution(1654953857427935169)
XLA Ops:
  7.5 3.8 collective-permute-start
  13.9 10.5 %collective-permute-done = bf16[6,3,512]{0,2,1:T(8,128)(2,1)S(1)} collective-permute-done((bf16[6,3,512]{0,2,1:T(8,128)(2,1)S(1)}, bf16[6,3,512]{0,2,1:T(8,128)(2,1)S(1)}, u32[]{:S(2)}, u32[]{:S(2)}) %collective-permute-start) | collective-permute-done | bytes 18464 | tf_op jit(solution)/shard_map/ppermute | solution.py:19
  24.7 3.0 fusion.2
  27.7 2.9 stack.2
  30.6 8.9 %all-to-all-start = ((bf16[32,128,512]{1,2,0:T(8,128)(2,1)}), bf16[32,128,512]{1,2,0:T(8,128)(2,1)}, u32[]{:S(2)}, u32[]{:S(2)}) async-start(bf16[32,128,512]{1,2,0:T(8,128)(2,1)} %stack.2), calls=%async_computation | async-start | bytes 8388608 | tf_op jit(solution)/shard_map/all_to_all | solution.py:11
  39.7 92.8 %all-to-all-done = bf16[32,128,512]{1,2,0:T(8,128)(2,1)} async-done(((bf16[32,128,512]{1,2,0:T(8,128)(2,1)}), bf16[32,128,512]{1,2,0:T(8,128)(2,1)}, u32[]{:S(2)}, u32[]{:S(2)}) %all-to-all-start) | async-done | bytes 4194336 | tf_op jit(solution)/shard_map/all_to_all | solution.py:11
  132.5 6.5 %copy.13 = bf16[32,128,512]{2,1,0:T(8,128)(2,1)} copy(bf16[32,128,512]{1,2,0:T(8,128)(2,1)} %all-to-all-done) | data formatting | bytes 8388608 | tf_op jit(solution)/shard_map/all_to_all | solution.py:11
  139.0 6.4 %copy.14 = bf16[4096,512]{0,1:T(8,128)(2,1)} copy(bf16[4096,512]{1,0:T(8,128)(2,1)} %bitcast.37) | data formatting | bytes 8388608 | tf_op jit(solution)/shard_map/while | solution.py:58
  145.4 117.9 %while.20 = (s32[]{:T(128)}, f32[128,512]{0,1:T(8,128)S(1)}, s32[]{:T(128)}, bf16[32,2560]{1,0:T(8,128)(2,1)S(1)}, bf16[4096,512]{0,1:T(8,128)(2,1)}, /*index=5*...) while((s32[]{:T(128)}, f32[128,512]{0,1:T(8,128)S(1)}, s32[]{:T(128)}, ...), condition=%wide.region_3.0_spmd, body=%wide.region_0.0_spmd.sunk | while | flops 16842768 | bytes 17285120 | solution.py:58
  145.5 12.9 %conditional.2 = (f32[128,512]{0,1:T(8,128)S(1)}) conditional(s32[]{:T(128)} %convert_element_type.43, f32[128,512]{0,1:T(8,128)S(1)} %get-tuple-element.304, (s32[]{:T(128)}, bf16[32,2560]{1,0:T(8,128)(2,1)S(1)}, s32[]{:T(128)}, bf16[4096,512]{0,1:T(8,128)(2,1)}, f32[128,512]{0,1:T(8,128)S(1)}) %tuple.79), branch_computations={%region_1.0_spmd, %region_2.0_spmd} | conditional | flops 16842760 | bytes 17284898 | solution.py:51
  148.3 7.8 %reshape.22 = bf16[32,128,255]{2,1,0:T(8,128)(2,1)} reshape(bf16[32,32640]{1,0:T(8,128)(2,1)S(1)} %slice.80) | data formatting | bytes 4177920 | tf_op jit(solution)/shard_map/while/body/eval_jaxpr/cond/branch_1_fun/reshape | solution.py:28
  158.4 12.9 %conditional.2 = (f32[128,512]{0,1:T(8,128)S(1)}) conditional(s32[]{:T(128)} %convert_element_type.43, f32[128,512]{0,1:T(8,128)S(1)} %get-tuple-element.304, (s32[]{:T(128)}, bf16[32,2560]{1,0:T(8,128)(2,1)S(1)}, s32[]{:T(128)}, bf16[4096,512]{0,1:T(8,128)(2,1)}, f32[128,512]{0,1:T(8,128)S(1)}) %tuple.79), branch_computations={%region_1.0_spmd, %region_2.0_spmd} | conditional | flops 16842760 | bytes 17284898 | solution.py:51
  161.2 7.8 %reshape.22 = bf16[32,128,255]{2,1,0:T(8,128)(2,1)} reshape(bf16[32,32640]{1,0:T(8,128)(2,1)S(1)} %slice.80) | data formatting | bytes 4177920 | tf_op jit(solution)/shard_map/while/body/eval_jaxpr/cond/branch_1_fun/reshape | solution.py:28
  171.4 12.9 %conditional.2 = (f32[128,512]{0,1:T(8,128)S(1)}) conditional(s32[]{:T(128)} %convert_element_type.43, f32[128,512]{0,1:T(8,128)S(1)} %get-tuple-element.304, (s32[]{:T(128)}, bf16[32,2560]{1,0:T(8,128)(2,1)S(1)}, s32[]{:T(128)}, bf16[4096,512]{0,1:T(8,128)(2,1)}, f32[128,512]{0,1:T(8,128)S(1)}) %tuple.79), branch_computations={%region_1.0_spmd, %region_2.0_spmd} | conditional | flops 16842760 | bytes 17284898 | solution.py:51
  174.2 7.8 %reshape.22 = bf16[32,128,255]{2,1,0:T(8,128)(2,1)} reshape(bf16[32,32640]{1,0:T(8,128)(2,1)S(1)} %slice.80) | data formatting | bytes 4177920 | tf_op jit(solution)/shard_map/while/body/eval_jaxpr/cond/branch_1_fun/reshape | solution.py:28
  182.0 2.3 fusion
  184.4 12.9 %conditional.2 = (f32[128,512]{0,1:T(8,128)S(1)}) conditional(s32[]{:T(128)} %convert_element_type.43, f32[128,512]{0,1:T(8,128)S(1)} %get-tuple-element.304, (s32[]{:T(128)}, bf16[32,2560]{1,0:T(8,128)(2,1)S(1)}, s32[]{:T(128)}, bf16[4096,512]{0,1:T(8,128)(2,1)}, f32[128,512]{0,1:T(8,128)S(1)}) %tuple.79), branch_computations={%region_1.0_spmd, %region_2.0_spmd} | conditional | flops 16842760 | bytes 17284898 | solution.py:51
  187.2 7.8 %reshape.22 = bf16[32,128,255]{2,1,0:T(8,128)(2,1)} reshape(bf16[32,32640]{1,0:T(8,128)(2,1)S(1)} %slice.80) | data formatting | bytes 4177920 | tf_op jit(solution)/shard_map/while/body/eval_jaxpr/cond/branch_1_fun/reshape | solution.py:28
  197.4 12.9 %conditional.2 = (f32[128,512]{0,1:T(8,128)S(1)}) conditional(s32[]{:T(128)} %convert_element_type.43, f32[128,512]{0,1:T(8,128)S(1)} %get-tuple-element.304, (s32[]{:T(128)}, bf16[32,2560]{1,0:T(8,128)(2,1)S(1)}, s32[]{:T(128)}, bf16[4096,512]{0,1:T(8,128)(2,1)}, f32[128,512]{0,1:T(8,128)S(1)}) %tuple.79), branch_computations={%region_1.0_spmd, %region_2.0_spmd} | conditional | flops 16842760 | bytes 17284898 | solution.py:51
  200.2 7.8 %reshape.22 = bf16[32,128,255]{2,1,0:T(8,128)(2,1)} reshape(bf16[32,32640]{1,0:T(8,128)(2,1)S(1)} %slice.80) | data formatting | bytes 4177920 | tf_op jit(solution)/shard_map/while/body/eval_jaxpr/cond/branch_1_fun/reshape | solution.py:28
  208.0 2.3 fusion
  210.4 12.9 %conditional.2 = (f32[128,512]{0,1:T(8,128)S(1)}) conditional(s32[]{:T(128)} %convert_element_type.43, f32[128,512]{0,1:T(8,128)S(1)} %get-tuple-element.304, (s32[]{:T(128)}, bf16[32,2560]{1,0:T(8,128)(2,1)S(1)}, s32[]{:T(128)}, bf16[4096,512]{0,1:T(8,128)(2,1)}, f32[128,512]{0,1:T(8,128)S(1)}) %tuple.79), branch_computations={%region_1.0_spmd, %region_2.0_spmd} | conditional | flops 16842760 | bytes 17284898 | solution.py:51
  213.2 7.8 %reshape.22 = bf16[32,128,255]{2,1,0:T(8,128)(2,1)} reshape(bf16[32,32640]{1,0:T(8,128)(2,1)S(1)} %slice.80) | data formatting | bytes 4177920 | tf_op jit(solution)/shard_map/while/body/eval_jaxpr/cond/branch_1_fun/reshape | solution.py:28
  220.9 2.3 fusion
  223.3 12.9 %conditional.2 = (f32[128,512]{0,1:T(8,128)S(1)}) conditional(s32[]{:T(128)} %convert_element_type.43, f32[128,512]{0,1:T(8,128)S(1)} %get-tuple-element.304, (s32[]{:T(128)}, bf16[32,2560]{1,0:T(8,128)(2,1)S(1)}, s32[]{:T(128)}, bf16[4096,512]{0,1:T(8,128)(2,1)}, f32[128,512]{0,1:T(8,128)S(1)}) %tuple.79), branch_computations={%region_1.0_spmd, %region_2.0_spmd} | conditional | flops 16842760 | bytes 17284898 | solution.py:51
  226.1 7.8 %reshape.22 = bf16[32,128,255]{2,1,0:T(8,128)(2,1)} reshape(bf16[32,32640]{1,0:T(8,128)(2,1)S(1)} %slice.80) | data formatting | bytes 4177920 | tf_op jit(solution)/shard_map/while/body/eval_jaxpr/cond/branch_1_fun/reshape | solution.py:28
  236.3 12.9 %conditional.2 = (f32[128,512]{0,1:T(8,128)S(1)}) conditional(s32[]{:T(128)} %convert_element_type.43, f32[128,512]{0,1:T(8,128)S(1)} %get-tuple-element.304, (s32[]{:T(128)}, bf16[32,2560]{1,0:T(8,128)(2,1)S(1)}, s32[]{:T(128)}, bf16[4096,512]{0,1:T(8,128)(2,1)}, f32[128,512]{0,1:T(8,128)S(1)}) %tuple.79), branch_computations={%region_1.0_spmd, %region_2.0_spmd} | conditional | flops 16842760 | bytes 17284898 | solution.py:51
  239.1 7.8 %reshape.22 = bf16[32,128,255]{2,1,0:T(8,128)(2,1)} reshape(bf16[32,32640]{1,0:T(8,128)(2,1)S(1)} %slice.80) | data formatting | bytes 4177920 | tf_op jit(solution)/shard_map/while/body/eval_jaxpr/cond/branch_1_fun/reshape | solution.py:28
  249.3 12.9 %conditional.2 = (f32[128,512]{0,1:T(8,128)S(1)}) conditional(s32[]{:T(128)} %convert_element_type.43, f32[128,512]{0,1:T(8,128)S(1)} %get-tuple-element.304, (s32[]{:T(128)}, bf16[32,2560]{1,0:T(8,128)(2,1)S(1)}, s32[]{:T(128)}, bf16[4096,512]{0,1:T(8,128)(2,1)}, f32[128,512]{0,1:T(8,128)S(1)}) %tuple.79), branch_computations={%region_1.0_spmd, %region_2.0_spmd} | conditional | flops 16842760 | bytes 17284898 | solution.py:51
  252.1 7.8 %reshape.22 = bf16[32,128,255]{2,1,0:T(8,128)(2,1)} reshape(bf16[32,32640]{1,0:T(8,128)(2,1)S(1)} %slice.80) | data formatting | bytes 4177920 | tf_op jit(solution)/shard_map/while/body/eval_jaxpr/cond/branch_1_fun/reshape | solution.py:28
  263.3 6.0 %convolution_convert_fusion = bf16[128,8192]{1,0:T(8,128)(2,1)} fusion(bf16[512,8192]{1,0:T(8,128)(2,1)} %param.11, f32[128,512]{0,1:T(8,128)S(1)} %get-tuple-element.232, f32[128,3,512]{0,2,1:T(8,128)S(1)} %fusion.2), kind=kOutput, calls=%fused_computation.5 | convolution fusion | flops 1074921472 | bytes 11010048 | tf_op jit(solution)/shard_map/dot_general | solution.py:81
  269.4 141.4 %reduce-scatter.2.cloned.1.call-done = bf16[128,1024]{1,0:T(8,128)(2,1)} async-done(((bf16[128,8192]{1,0:T(8,128)(2,1)}), bf16[128,1024]{1,0:T(8,128)(2,1)}) %reduce-scatter.2.cloned.1.call-update) | async-done | bytes 262160 | tf_op jit(solution)/shard_map/reduce_scatter | solution.py:82
  (127 shorter events, 43.2 us)
Async XLA Ops:
  7.5 16.8 %collective-permute-start = (bf16[6,3,512]{0,2,1:T(8,128)(2,1)S(1)}, bf16[6,3,512]{0,2,1:T(8,128)(2,1)S(1)}, u32[]{:S(2)}, u32[]{:S(2)}) collective-permute-start(bf16[6,3,512]{0,2,1:T(8,128)(2,1)S(1)} %copy.11), channel_id=1, source_target_pairs={{0,8},{8,16},{16,24},{24,32},{32,40},{40,48},{48,56},{56,64},{64,7... | collective-permute-start | bytes 55304 | tf_op jit(solution)/shard_map/ppermute | solution.py:19
  30.6 9.0 %copy-start = (bf16[32,2048]{1,0:T(8,128)(2,1)S(1)}, bf16[32,2048]{1,0:T(8,128)(2,1)}, u32[]{:S(2)}) copy-start(bf16[32,2048]{1,0:T(8,128)(2,1)} %param.10) | copy-start | bytes 393220
  30.6 101.9 %all-to-all-start = ((bf16[32,128,512]{1,2,0:T(8,128)(2,1)}), bf16[32,128,512]{1,2,0:T(8,128)(2,1)}, u32[]{:S(2)}, u32[]{:S(2)}) async-start(bf16[32,128,512]{1,2,0:T(8,128)(2,1)} %stack.2), calls=%async_computation | async-start | bytes 8388608 | tf_op jit(solution)/shard_map/all_to_all | solution.py:11
  39.6 371.2 %reduce-scatter.2.cloned.1.call-start = ((), (), s32[]{:S(2)}) async-start(), calls=%async_computation.2 | async-start | bytes 2359296 | tf_op jit(solution)/shard_map/reduce_scatter | solution.py:82
Sparse Core Ops, SparseCore 0:
  269.5 141.2 reduce-scatter.1
